TPU v7x, 512 devices: a whole 4x8x8 slice. The times are simulated.
512 devices in a mesh: energy: 32 (over y, z_lo, core), slab: 16 (over x, z_hi).
Axes of the slice: x: 4, y: 8, z: 8 (z_hi: 4, z_lo: 2; z = z_hi * 2 + z_lo), core: 2. Of those that a mesh axis runs over, the one named last changes fastest.
Arguments:
- green_lesser: float32 [64, 16, 2, 128, 128], P('energy', 'slab'), may hold values from -6 to 6
- coupling: float32 [4, 16, 3, 2, 128, 128], P(None, 'slab'), may hold values from -0.375 to 0.375
- occupation: float32 [4], replicated, may hold values from 0.2 to 3
- shifts: int32 [4], replicated, may hold values from 1 to 2, as said below
- neighbours: int32 [16, 3], P('slab'), may hold values from 0 to 15, as said below
Outputs:
- self_energy: float32 [64, 16, 2, 128, 128], P('energy', 'slab')
Inputs may be any that keep to these rules, and one draw needn't show every extreme that they name: `shifts`: some mode's shift is 1 and some mode's shift is 2. `neighbours`: entry 0 of row i is max(i - 1, 0), entry 2 is min(i + 1, 15), entry 1 lies within one of i.
All inputs are finite; a program needn't handle non-finite values.
Results may differ from a plain program's by a relative error of at most 0.0001.
Values sent between devices are 32-bit elements; how exact they have to be, the bound alone decides.
A program may use at most 64 MiB of HBM per device.

v0:
```python
import jax
import jax.numpy as jnp
from jax import lax
from jax.sharding import PartitionSpec as P


def passed_along(value, axis, steps):
    count = lax.axis_size(axis)
    leading, last = (max(0, -steps), min(count, count - steps))
    return lax.ppermute(value, axis, [(source, source + steps) for source in range(leading, last)])


def padded(block, sides, width):
    for axis, dim in sides:
        count = lax.axis_size(axis)
        forward = [(i, i + 1) for i in range(count - 1)]
        backward = [(target, source) for source, target in forward]
        low = lax.ppermute(
            lax.slice_in_dim(block, block.shape[dim] - width, None, axis=dim), axis, forward
        )
        high = lax.ppermute(lax.slice_in_dim(block, 0, width, axis=dim), axis, backward)
        block = jnp.concatenate([low, block, high], axis=dim)
    return block


def precise_matmul(first, second):
    return jnp.matmul(first, second, precision=lax.Precision.HIGHEST)


def complex_product(leading, trailing):
    lead_real, lead_imag = (leading[..., 0, :, :], leading[..., 1, :, :])
    trail_real, trail_imag = (trailing[..., 0, :, :], trailing[..., 1, :, :])
    real_part = precise_matmul(lead_real, trail_real) - precise_matmul(lead_imag, trail_imag)
    imag_part = precise_matmul(lead_real, trail_imag) + precise_matmul(lead_imag, trail_real)
    return jnp.stack([real_part, imag_part], axis=-3)


def adjoint_product(leading, trailing):
    lead_real, lead_imag = (leading[..., 0, :, :], leading[..., 1, :, :])
    trail_real = jnp.swapaxes(trailing[..., 0, :, :], -1, -2)
    trail_imag = jnp.swapaxes(trailing[..., 1, :, :], -1, -2)
    real_part = precise_matmul(lead_real, trail_real) + precise_matmul(lead_imag, trail_imag)
    imag_part = precise_matmul(lead_imag, trail_real) - precise_matmul(lead_real, trail_imag)
    return jnp.stack([real_part, imag_part], axis=-3)


def sandwich(couple, middle):
    return adjoint_product(complex_product(couple, middle), couple)


def shards(green_lesser, coupling, occupation, shifts, neighbours):
    energy_count = green_lesser.shape[0]
    block_count = green_lesser.shape[1]
    shifted = [passed_along(green_lesser, "energy", offset_step) for offset_step in (1, -1)]
    extended = jnp.concatenate([shifted[0], green_lesser, shifted[1]], axis=0)
    gathered_blocks = padded(extended, (("slab", 1),), 1)
    position = neighbours - lax.axis_index("slab") * block_count + 1
    local_energy = jnp.arange(energy_count, dtype=jnp.int32) + energy_count
    summed = jnp.zeros_like(green_lesser)
    for mode_index in range(coupling.shape[0]):
        shift_now = shifts[mode_index]
        source = jnp.stack([local_energy + shift_now, local_energy - shift_now], axis=1)
        chosen = gathered_blocks[source[:, :, None, None], position[None, None, :, :]]
        couple = coupling[mode_index]
        weights = jnp.stack([occupation[mode_index] + 1.0, occupation[mode_index]])
        weighted = weights[0] * chosen[:, 0] + weights[1] * chosen[:, 1]
        summed = summed + jnp.sum(sandwich(couple[None], weighted), axis=2)
    return summed


def solution(mesh):
    placed = (
        P("energy", "slab", None, None, None),
        P(None, "slab", None, None, None, None),
        P(),
        P(),
        P("slab", None),
    )
    return jax.shard_map(
        shards,
        mesh=mesh,
        in_specs=placed,
        out_specs=P("energy", "slab", None, None, None),
        check_vma=False,
    )
```

profile of v0, /device:TPU:30, one launch (start us, length us, event | category | flops | bytes accessed | tf_op | source)
XLA Modules:
  0.0 141.2 jit_solution(6446504142315166629)
XLA Ops:
  0.0 2.0 %collective-permute-start = (f32[2,1,2,128,128]{4,3,2,1,0:T(8,128)}, f32[2,1,2,128,128]{4,3,2,1,0:T(8,128)S(1)}, u32[]{:S(2)}, u32[]{:S(2)}) collective-permute-start(f32[2,1,2,128,128]{4,3,2,1,0:T(8,128)} %param.5), channel_id=1, source_target_pairs={{0,16},{16,32},{32,48},{48,64},{64,80},{80,96},{96,112},{112,128},... | collective-permute-start | bytes 786440 | tf_op jit(solution)/shard_map/ppermute | solution.py:10
  2.1 4.5 %collective-permute-start.1 = (f32[2,1,2,128,128]{4,3,2,1,0:T(8,128)}, f32[2,1,2,128,128]{4,3,2,1,0:T(8,128)S(1)}, u32[]{:S(2)}, u32[]{:S(2)}) collective-permute-start(f32[2,1,2,128,128]{4,3,2,1,0:T(8,128)} %param.5), channel_id=1, source_target_pairs={{16,0},{32,16},{48,32},{64,48},{80,64},{96,80},{112,96},{128,112},... | collective-permute-start | bytes 786440 | tf_op jit(solution)/shard_map/ppermute | solution.py:10
  6.6 1.5 %fusion.129 = (s32[1]{0:T(128)}, s32[1]{0:T(128)}, s32[1]{0:T(128)}, s32[1]{0:T(128)}) fusion(s32[4]{0:T(128)} %param.8), kind=kLoop, calls=%fused_computation.188 | loop fusion | bytes 32 | tf_op jit(solution)/shard_map/slice | solution.py:61
  13.3 1.5 %fusion.128 = (f32[1]{0:T(128)}, f32[1]{0:T(128)}, f32[1]{0:T(128)}, f32[1]{0:T(128)}) fusion(f32[4]{0:T(128)} %param.7), kind=kLoop, calls=%fused_computation.187 | loop fusion | bytes 32 | tf_op jit(solution)/shard_map/slice | solution.py:65
  18.6 11.2 %collective-permute-start.3 = (f32[6,1,2,128,128]{4,3,2,1,0:T(8,128)S(1)}, f32[6,1,2,128,128]{4,3,2,1,0:T(8,128)S(1)}, u32[]{:S(2)}, u32[]{:S(2)}) collective-permute-start(f32[6,1,2,128,128]{4,3,2,1,0:T(8,128)S(1)} %constant_dynamic-update-slice_fusion), channel_id=1, source_target_pairs={{1,0},{2,1},{3,2},{4,3},{5,4},{6,5},{7,6},{8,7},{9,8},{10,9},{11,1... | collective-permute-start | bytes 2359304 | tf_op jit(solution)/shard_map/ppermute | solution.py:21
  29.8 1.9 %collective-permute-start.2 = (f32[6,1,2,128,128]{4,3,2,1,0:T(8,128)S(1)}, f32[6,1,2,128,128]{4,3,2,1,0:T(8,128)}, u32[]{:S(2)}, u32[]{:S(2)}) collective-permute-start(f32[6,1,2,128,128]{4,3,2,1,0:T(8,128)S(1)} %constant_dynamic-update-slice_fusion), channel_id=1, source_target_pairs={{0,1},{1,2},{2,3},{3,4},{4,5},{5,6},{6,7},{7,8},{8,9},{9,10},{10,1... | collective-permute-start | bytes 2359304 | tf_op jit(solution)/shard_map/ppermute | solution.py:18
  32.6 30.0 %collective-permute-done.3 = f32[6,1,2,128,128]{4,3,2,1,0:T(8,128)S(1)} collective-permute-done((f32[6,1,2,128,128]{4,3,2,1,0:T(8,128)S(1)}, f32[6,1,2,128,128]{4,3,2,1,0:T(8,128)S(1)}, u32[]{:S(2)}, u32[]{:S(2)}) %collective-permute-start.3) | collective-permute-done | bytes 786464 | tf_op jit(solution)/shard_map/ppermute | solution.py:21
  63.5 6.3 %collective-permute-done.2 = f32[6,1,2,128,128]{4,3,2,1,0:T(8,128)} collective-permute-done((f32[6,1,2,128,128]{4,3,2,1,0:T(8,128)S(1)}, f32[6,1,2,128,128]{4,3,2,1,0:T(8,128)}, u32[]{:S(2)}, u32[]{:S(2)}) %collective-permute-start.2) | collective-permute-done | bytes 786464 | tf_op jit(solution)/shard_map/ppermute | solution.py:18
  69.8 1.5 %pad_maximum_fusion = f32[6,3,2,128,128]{4,3,2,1,0:T(8,128)S(1)} fusion(f32[6,1,2,128,128]{4,3,2,1,0:T(8,128)} %copy-done.10, f32[6,1,2,128,128]{4,3,2,1,0:T(8,128)S(1)} %constant_dynamic-update-slice_fusion, f32[6,1,2,128,128]{4,3,2,1,0:T(8,128)} %collective-permute-done.2), kind=kLoop, calls=%fused_computation.4 | loop fusion | flops 1179648 | bytes 4718592 | tf_op jit(solution)/shard_map/concatenate | solution.py:22
  71.3 1.9 %gather_fusion.3 = f32[12,2,128,128]{3,2,1,0:T(8,128)} fusion(f32[6,3,2,128,128]{4,3,2,1,0:T(8,128)S(1)} %pad_maximum_fusion, s32[12]{0:T(128)S(1)} %reshape.427), kind=kCustom, calls=%fused_computation.3 | custom fusion | bytes 3145824 | tf_op jit(solution)/shard_map/gather | solution.py:63
  73.2 2.4 %fusion.127 = (f32[2,1,1,3,2,128,128]{6,5,4,3,1,0,2:T(8,128)}, f32[2,1,1,3,2,128,128]{6,5,4,3,1,0,2:T(8,128)S(1)}) fusion(f32[2,2,1,3,2,128,128]{6,5,4,3,1,0,2:T(8,128)} %bitcast.337), kind=kLoop, calls=%fused_computation.186 | loop fusion | bytes 3145728 | tf_op jit(solution)/shard_map/slice | solution.py:66
  75.6 2.3 %copy.227 = f32[2,1,1,3,2,128,128]{5,6,0,3,4,2,1:T(8,128)} copy(f32[2,1,1,3,2,128,128]{6,5,4,3,1,0,2:T(8,128)} %get-tuple-element.11) | data formatting | bytes 1572864
  77.9 1.2 copy.228
  79.0 2.1 %add_bitcast_fusion = f32[2,1,3,2,128,128]{4,5,0,2,3,1:T(8,128)S(1)} fusion(f32[2,1,1,3,2,128,128]{5,6,0,3,4,2,1:T(8,128)} %copy.228, f32[2,1,1,3,2,128,128]{5,6,0,3,4,2,1:T(8,128)} %copy.227, f32[]{:T(128)} %bitcast.112, f32[]{:T(128)S(6)} %add.393), kind=kLoop, calls=%fused_computation.41 | loop fusion | flops 589824 | bytes 2359304 | tf_op jit(solution)/shard_map/add | solution.py:66
  81.2 2.2 %fusion.23 = f32[3,2,128,128]{3,2,1,0:T(8,128)} fusion(f32[2,1,3,2,128,128]{4,5,0,2,3,1:T(8,128)S(1)} %add_bitcast_fusion, f32[4,1,3,2,128,128]{5,4,3,2,1,0:T(8,128)} %param.6), kind=kOutput, calls=%fused_computation.60 | convolution fusion | flops 150994944 | bytes 983040 | tf_op jit(solution)/shard_map/dot_general | solution.py:27
  83.4 1.4 %fusion.22 = f32[3,2,128,128]{3,2,1,0:T(8,128)S(1)} fusion(f32[2,1,3,2,128,128]{4,5,0,2,3,1:T(8,128)S(1)} %add_bitcast_fusion, f32[4,1,3,2,128,128]{5,4,3,2,1,0:T(8,128)} %param.6), kind=kOutput, calls=%fused_computation.59 | convolution fusion | flops 150994944 | bytes 983040 | tf_op jit(solution)/shard_map/dot_general | solution.py:27
  84.8 1.9 %gather_fusion.2 = f32[12,2,128,128]{3,2,1,0:T(8,128)} fusion(f32[6,3,2,128,128]{4,3,2,1,0:T(8,128)S(1)} %pad_maximum_fusion, s32[12]{0:T(128)S(1)} %reshape.419), kind=kCustom, calls=%fused_computation.2 | custom fusion | bytes 3145824 | tf_op jit(solution)/shard_map/gather | solution.py:63
  86.6 2.7 %fusion.126 = (f32[2,1,1,3,2,128,128]{6,5,4,3,1,0,2:T(8,128)}, f32[2,1,1,3,2,128,128]{6,5,4,3,1,0,2:T(8,128)}) fusion(f32[2,2,1,3,2,128,128]{6,5,4,3,1,0,2:T(8,128)} %bitcast.338), kind=kLoop, calls=%fused_computation.185 | loop fusion | bytes 3145728 | tf_op jit(solution)/shard_map/slice | solution.py:66
  89.3 2.3 %copy.223 = f32[2,1,1,3,2,128,128]{5,6,0,3,4,2,1:T(8,128)} copy(f32[2,1,1,3,2,128,128]{6,5,4,3,1,0,2:T(8,128)} %get-tuple-element.9) | data formatting | bytes 1572864
  91.6 2.3 %copy.224 = f32[2,1,1,3,2,128,128]{5,6,0,3,4,2,1:T(8,128)} copy(f32[2,1,1,3,2,128,128]{6,5,4,3,1,0,2:T(8,128)} %get-tuple-element.10) | data formatting | bytes 1572864
  93.9 2.1 %add_bitcast_fusion.1 = f32[2,1,3,2,128,128]{4,5,0,2,3,1:T(8,128)S(1)} fusion(f32[2,1,1,3,2,128,128]{5,6,0,3,4,2,1:T(8,128)} %copy.224, f32[2,1,1,3,2,128,128]{5,6,0,3,4,2,1:T(8,128)} %copy.223, f32[]{:T(128)} %bitcast.75, f32[]{:T(128)S(6)} %add.382), kind=kLoop, calls=%fused_computation.42 | loop fusion | flops 589824 | bytes 2359304 | tf_op jit(solution)/shard_map/add | solution.py:66
  96.1 2.4 %fusion.21 = f32[3,2,128,128]{3,2,1,0:T(8,128)} fusion(f32[2,1,3,2,128,128]{4,5,0,2,3,1:T(8,128)S(1)} %add_bitcast_fusion.1, f32[4,1,3,2,128,128]{5,4,3,2,1,0:T(8,128)} %param.6), kind=kOutput, calls=%fused_computation.58 | convolution fusion | flops 150994944 | bytes 983040 | tf_op jit(solution)/shard_map/dot_general | solution.py:27
  98.5 2.2 %fusion.20 = f32[3,2,128,128]{3,2,1,0:T(8,128)} fusion(f32[2,1,3,2,128,128]{4,5,0,2,3,1:T(8,128)S(1)} %add_bitcast_fusion.1, f32[4,1,3,2,128,128]{5,4,3,2,1,0:T(8,128)} %param.6), kind=kOutput, calls=%fused_computation.57 | convolution fusion | flops 150994944 | bytes 983040 | tf_op jit(solution)/shard_map/dot_general | solution.py:27
  100.7 1.9 %gather_fusion = f32[12,2,128,128]{3,2,1,0:T(8,128)} fusion(f32[6,3,2,128,128]{4,3,2,1,0:T(8,128)S(1)} %pad_maximum_fusion, s32[12]{0:T(128)S(1)} %reshape.403), kind=kCustom, calls=%fused_computation | custom fusion | bytes 3145824 | tf_op jit(solution)/shard_map/gather | solution.py:63
  102.5 2.7 %fusion.125 = (f32[2,1,1,3,2,128,128]{6,5,4,3,1,0,2:T(8,128)}, f32[2,1,1,3,2,128,128]{6,5,4,3,1,0,2:T(8,128)}) fusion(f32[2,2,1,3,2,128,128]{6,5,4,3,1,0,2:T(8,128)} %bitcast.339), kind=kLoop, calls=%fused_computation.184 | loop fusion | bytes 3145728 | tf_op jit(solution)/shard_map/slice | solution.py:66
  105.2 2.3 %copy.215 = f32[2,1,1,3,2,128,128]{5,6,0,3,4,2,1:T(8,128)} copy(f32[2,1,1,3,2,128,128]{6,5,4,3,1,0,2:T(8,128)} %get-tuple-element.7) | data formatting | bytes 1572864
  107.5 2.3 %copy.216 = f32[2,1,1,3,2,128,128]{5,6,0,3,4,2,1:T(8,128)} copy(f32[2,1,1,3,2,128,128]{6,5,4,3,1,0,2:T(8,128)} %get-tuple-element.8) | data formatting | bytes 1572864
  109.8 2.1 %add_bitcast_fusion.3 = f32[2,1,3,2,128,128]{4,5,0,2,3,1:T(8,128)S(1)} fusion(f32[2,1,1,3,2,128,128]{5,6,0,3,4,2,1:T(8,128)} %copy.216, f32[2,1,1,3,2,128,128]{5,6,0,3,4,2,1:T(8,128)} %copy.215, f32[]{:T(128)} %bitcast, f32[]{:T(128)S(6)} %add.358), kind=kLoop, calls=%fused_computation.44 | loop fusion | flops 589824 | bytes 2359304 | tf_op jit(solution)/shard_map/add | solution.py:66
  111.9 2.4 %fusion.17 = f32[3,2,128,128]{3,2,1,0:T(8,128)} fusion(f32[2,1,3,2,128,128]{4,5,0,2,3,1:T(8,128)S(1)} %add_bitcast_fusion.3, f32[4,1,3,2,128,128]{5,4,3,2,1,0:T(8,128)} %param.6), kind=kOutput, calls=%fused_computation.54 | convolution fusion | flops 150994944 | bytes 983040 | tf_op jit(solution)/shard_map/dot_general | solution.py:27
  114.3 2.1 %fusion.16 = f32[3,2,128,128]{3,2,1,0:T(8,128)} fusion(f32[2,1,3,2,128,128]{4,5,0,2,3,1:T(8,128)S(1)} %add_bitcast_fusion.3, f32[4,1,3,2,128,128]{5,4,3,2,1,0:T(8,128)} %param.6), kind=kOutput, calls=%fused_computation.53 | convolution fusion | flops 150994944 | bytes 983040 | tf_op jit(solution)/shard_map/dot_general | solution.py:27
  116.5 1.9 %gather_fusion.1 = f32[12,2,128,128]{3,2,1,0:T(8,128)} fusion(f32[6,3,2,128,128]{4,3,2,1,0:T(8,128)S(1)} %pad_maximum_fusion, s32[12]{0:T(128)S(1)} %reshape.411), kind=kCustom, calls=%fused_computation.1 | custom fusion | bytes 3145824 | tf_op jit(solution)/shard_map/gather | solution.py:63
  118.3 1.5 %fusion.124 = (f32[2,1,1,3,2,128,128]{6,5,4,3,1,0,2:T(8,128)S(1)}, f32[2,1,1,3,2,128,128]{6,5,4,3,1,0,2:T(8,128)S(1)}) fusion(f32[2,2,1,3,2,128,128]{6,5,4,3,1,0,2:T(8,128)} %bitcast.336), kind=kLoop, calls=%fused_computation.183 | loop fusion | bytes 3145728 | tf_op jit(solution)/shard_map/slice | solution.py:66
  (89 shorter events, 29.0 us)
Async XLA Ops:
  0.0 31.9 %copy-start.11 = (s32[1,3]{1,0:T(1,128)S(1)}, s32[1,3]{1,0:T(1,128)}, u32[]{:S(2)}) copy-start(s32[1,3]{1,0:T(1,128)} %param.9) | copy-start | bytes 40
  0.0 17.5 %collective-permute-start = (f32[2,1,2,128,128]{4,3,2,1,0:T(8,128)}, f32[2,1,2,128,128]{4,3,2,1,0:T(8,128)S(1)}, u32[]{:S(2)}, u32[]{:S(2)}) collective-permute-start(f32[2,1,2,128,128]{4,3,2,1,0:T(8,128)} %param.5), channel_id=1, source_target_pairs={{0,16},{16,32},{32,48},{48,64},{64,80},{80,96},{96,112},{112,128},... | collective-permute-start | bytes 786440 | tf_op jit(solution)/shard_map/ppermute | solution.py:10
  2.1 16.5 %collective-permute-start.1 = (f32[2,1,2,128,128]{4,3,2,1,0:T(8,128)}, f32[2,1,2,128,128]{4,3,2,1,0:T(8,128)S(1)}, u32[]{:S(2)}, u32[]{:S(2)}) collective-permute-start(f32[2,1,2,128,128]{4,3,2,1,0:T(8,128)} %param.5), channel_id=1, source_target_pairs={{16,0},{32,16},{48,32},{64,48},{80,64},{96,80},{112,96},{128,112},... | collective-permute-start | bytes 786440 | tf_op jit(solution)/shard_map/ppermute | solution.py:10
  18.6 44.0 %collective-permute-start.3 = (f32[6,1,2,128,128]{4,3,2,1,0:T(8,128)S(1)}, f32[6,1,2,128,128]{4,3,2,1,0:T(8,128)S(1)}, u32[]{:S(2)}, u32[]{:S(2)}) collective-permute-start(f32[6,1,2,128,128]{4,3,2,1,0:T(8,128)S(1)} %constant_dynamic-update-slice_fusion), channel_id=1, source_target_pairs={{1,0},{2,1},{3,2},{4,3},{5,4},{6,5},{7,6},{8,7},{9,8},{10,9},{11,1... | collective-permute-start | bytes 2359304 | tf_op jit(solution)/shard_map/ppermute | solution.py:21
  29.8 40.0 %collective-permute-start.2 = (f32[6,1,2,128,128]{4,3,2,1,0:T(8,128)S(1)}, f32[6,1,2,128,128]{4,3,2,1,0:T(8,128)}, u32[]{:S(2)}, u32[]{:S(2)}) collective-permute-start(f32[6,1,2,128,128]{4,3,2,1,0:T(8,128)S(1)} %constant_dynamic-update-slice_fusion), channel_id=1, source_target_pairs={{0,1},{1,2},{2,3},{3,4},{4,5},{5,6},{6,7},{7,8},{8,9},{9,10},{10,1... | collective-permute-start | bytes 2359304 | tf_op jit(solution)/shard_map/ppermute | solution.py:18
  62.6 0.9 copy-start.10
  96.1 2.4 %copy-start.1 = (f32[2,1,3,2,128,128]{4,5,0,2,3,1:T(8,128)}, f32[2,1,3,2,128,128]{4,5,0,2,3,1:T(8,128)S(1)}, u32[]{:S(2)}) copy-start(f32[2,1,3,2,128,128]{4,5,0,2,3,1:T(8,128)S(1)} %add_bitcast_fusion.1) | copy-start | bytes 2359300
  111.9 2.4 %copy-start.3 = (f32[2,1,3,2,128,128]{4,5,0,2,3,1:T(8,128)}, f32[2,1,3,2,128,128]{4,5,0,2,3,1:T(8,128)S(1)}, u32[]{:S(2)}) copy-start(f32[2,1,3,2,128,128]{4,5,0,2,3,1:T(8,128)S(1)} %add_bitcast_fusion.3) | copy-start | bytes 2359300
  120.4 1.4 %copy-start = (f32[4,1,3,2,128,128]{5,4,3,2,1,0:T(8,128)S(1)}, f32[4,1,3,2,128,128]{5,4,3,2,1,0:T(8,128)}, u32[]{:S(2)}) copy-start(f32[4,1,3,2,128,128]{5,4,3,2,1,0:T(8,128)} %param.6) | copy-start | bytes 4718596
  121.8 1.0 copy-start.5
  125.4 1.7 %copy-start.2 = (f32[2,1,3,2,128,128]{4,5,0,2,3,1:T(8,128)S(1)}, f32[2,1,3,2,128,128]{4,5,0,2,3,1:T(8,128)}, u32[]{:S(2)}) copy-start(f32[2,1,3,2,128,128]{4,5,0,2,3,1:T(8,128)} %copy-done.1) | copy-start | bytes 2359300
  125.4 1.7 %copy-start.7 = (f32[3,2,128,128]{3,2,1,0:T(8,128)S(1)}, f32[3,2,128,128]{3,2,1,0:T(8,128)}, u32[]{:S(2)}) copy-start(f32[3,2,128,128]{3,2,1,0:T(8,128)} %fusion.21) | copy-start | bytes 1179652
  126.3 2.3 %copy-start.6 = (f32[3,2,128,128]{3,2,1,0:T(8,128)S(1)}, f32[3,2,128,128]{3,2,1,0:T(8,128)}, u32[]{:S(2)}) copy-start(f32[3,2,128,128]{3,2,1,0:T(8,128)} %fusion.20) | copy-start | bytes 1179652
  129.9 1.7 %copy-start.4 = (f32[2,1,3,2,128,128]{4,5,0,2,3,1:T(8,128)S(1)}, f32[2,1,3,2,128,128]{4,5,0,2,3,1:T(8,128)}, u32[]{:S(2)}) copy-start(f32[2,1,3,2,128,128]{4,5,0,2,3,1:T(8,128)} %copy-done.3) | copy-start | bytes 2359300
  129.9 1.7 %copy-start.9 = (f32[3,2,128,128]{3,2,1,0:T(8,128)S(1)}, f32[3,2,128,128]{3,2,1,0:T(8,128)}, u32[]{:S(2)}) copy-start(f32[3,2,128,128]{3,2,1,0:T(8,128)} %fusion.17) | copy-start | bytes 1179652
  130.8 2.2 %copy-start.8 = (f32[3,2,128,128]{3,2,1,0:T(8,128)S(1)}, f32[3,2,128,128]{3,2,1,0:T(8,128)}, u32[]{:S(2)}) copy-start(f32[3,2,128,128]{3,2,1,0:T(8,128)} %fusion.16) | copy-start | bytes 1179652
where the time goes:
time: 142 us; the launch traced here: 141 us
  local copies, waits for them, and re-layouts  36.6 us (26%)
  waiting for transfers between devices  36.3 us (26%)
  matrix products  30.8 us (22%)
  starting transfers between devices  19.7 us (14%)
  other arithmetic  14.5 us (10%)
  between operations  3.27 us (2%)
    dot_general x32, matrix products, precise_matmul(): return jnp.matmul(first, second, precision=lax.Precision.HIGHEST)  30.8 us
    ppermute x1, waiting for transfers between devices, padded(): lax.ppermute(lax.slice_in_dim(block, 0, width, axis=dim), axis, backward)  30 us
    unnamed x34, local copies, waits for them, and re-layouts  15.6 us
    ppermute x1, starting transfers between devices, padded(): lax.ppermute(lax.slice_in_dim(block, 0, width, axis=dim), axis, backward)  11.2 us
    slice x4, local copies, waits for them, and re-layouts, shards(): weighted = weights[0] * chosen[:, 0] + weights[1] * chosen[:, 1]  9.26 us
    gather x4, local copies, waits for them, and re-layouts, shards(): gathered_blocks[source[:, :, None, None], position[None, None, :, :]]  7.42 us
    add x4, other arithmetic, shards(): weighted = weights[0] * chosen[:, 0] + weights[1] * chosen[:, 1]  7.28 us
    ppermute x2, starting transfers between devices, passed_along(): lax.ppermute(value, axis, [(source, source + steps) for source in range(l...  6.59 us
  transfers between devices with their start and end apart: 4, of which 2 were waited for; matrix products, arithmetic and copies ran while one was open for 7% of the time, Pallas kernels for 0%

commit v1 on v0

v1 whole, which is shorter than its diff:
```python
import functools

import jax
import jax.numpy as jnp
from jax import lax
from jax.experimental import pallas as pl
from jax.experimental.pallas import tpu as pltpu
from jax.sharding import PartitionSpec as P

MESH = pl.DeviceIdType.MESH
CHUNKS = 4
AHEAD = 2
OWN = 1


def halves(value):
    high = value.astype(jnp.bfloat16)
    return high, (value - high.astype(jnp.float32)).astype(jnp.bfloat16)


def kernel(energy_count, energies, slabs, occ_ref, shift_ref, near_ref, g_ref, c_ref, out_ref, *scratch):
    bufs = scratch[:CHUNKS]
    couple, adjoint_high, adjoint_low, left = scratch[CHUNKS : CHUNKS + 4]
    middle_high, middle_low, total = scratch[CHUNKS + 4 : CHUNKS + 7]
    send_sem, recv_sem, own_sem, couple_sem, ready_sem = scratch[CHUNKS + 7 :]
    modes, ks = c_ref.shape[0], c_ref.shape[2]
    size = c_ref.shape[-1]
    rows = size // CHUNKS

    a, s = lax.axis_index("energy"), lax.axis_index("slab")
    core, layer = lax.rem(a, 2), lax.rem(lax.div(a, 2), 2)
    step = 2 * core - 1

    def ring(value, count):
        return lax.rem(value + count, count)

    outer, partner = ring(a + step, energies), ring(a - step, energies)
    across = jnp.where(layer == 0, s - 1, s + 1)
    close = 2 - 2 * layer
    far = 2 * layer
    has_far = (across >= 0) & (across < slabs)
    has_close = (2 * s - across >= 0) & (2 * s - across < slabs)

    def own_block(r):
        return g_ref.at[:, 0, :, pl.ds(r * rows, rows), :]

    def slot(r, side, place):
        return bufs[r].at[side, pl.ds(2 * place, 2)]

    def remote(flow, r, source, side, place, target):
        return pltpu.make_async_remote_copy(
            src_ref=source,
            dst_ref=slot(r, side, place),
            send_sem=send_sem.at[flow, r],
            recv_sem=recv_sem.at[r, side, place],
            device_id={"energy": target[0], "slab": target[1]},
            device_id_type=MESH,
        )

    def flow_copy(flow, r):
        own = own_block(r)
        table = (
            (own, OWN, 1 - step, (outer, s)),
            (own, OWN, 1 + step, (partner, s)),
            (own, close, 1 - step, (outer, across)),
            (slot(r, OWN, 1 + step), close, 1, (outer, across)),
            (slot(r, far, 1 + step), far, 1, (outer, s)),
            (slot(r, far, 1), far, 1 - step, (outer, s)),
            (slot(r, far, 1), far, 1 + step, (partner, s)),
            (slot(r, close, 1), close, 1 + step, (partner, s)),
        )
        return remote(flow, r, *table[flow])

    def arrived(r, side, place):
        remote(0, r, slot(r, side, place), side, place, (outer, s)).wait_recv()

    couple_copy = pltpu.make_async_copy(c_ref, couple, couple_sem)
    couple_copy.start()

    def signal(semaphore, target):
        pl.semaphore_signal(
            semaphore, inc=1, device_id={"energy": target[0], "slab": target[1]}, device_id_type=MESH
        )

    barrier = pltpu.get_barrier_semaphore()
    signal(barrier, (outer, s))
    signal(barrier, (partner, s))

    @pl.when((layer == 0) & has_far)
    def _():
        signal(barrier, (outer, across))

    own_copies = [
        pltpu.make_async_copy(own_block(r), slot(r, OWN, 1), own_sem.at[r]) for r in range(CHUNKS)
    ]
    for copy in own_copies:
        copy.start()
    pl.semaphore_wait(barrier, jnp.where((layer == 1) & has_far, 3, 2))

    @pl.when((layer == 1) & has_far)
    def _():
        signal(ready_sem, (outer, across))
        for r in range(AHEAD):
            flow_copy(2, r).start()

    for r in range(CHUNKS):
        flow_copy(0, r).start()
        flow_copy(1, r).start()

    def prepare():
        couple_copy.wait()

        def mode_step(m, _):
            for k in range(ks):
                real, imag = couple[m, 0, k, 0], couple[m, 0, k, 1]
                real_t, imag_t = real.T, imag.T
                adjoint = jnp.concatenate(
                    [
                        jnp.concatenate([real_t, -imag_t], axis=1),
                        jnp.concatenate([imag_t, real_t], axis=1),
                    ],
                    axis=0,
                )
                high, low = halves(adjoint)
                adjoint_high[m, k] = high
                adjoint_low[m, k] = low
            return 0

        lax.fori_loop(0, modes, mode_step, 0)
        for r in range(CHUNKS):
            for k in range(ks):
                stacked = jnp.concatenate(
                    [
                        couple[m, 0, k, part][:, r * rows : (r + 1) * rows]
                        for m in range(modes)
                        for part in range(2)
                    ],
                    axis=1,
                )
                high, low = halves(stacked)
                left[r, k, :size] = high
                left[r, k, size:] = low

    def relay_far(r):
        arrived(r, OWN, 1 + step)

        @pl.when(has_far)
        def _():
            flow_copy(3, r).start()
            if r + AHEAD < CHUNKS:
                flow_copy(2, r + AHEAD).start()
            arrived(r, far, 1 + step)
            flow_copy(4, r).start()

    def relay_close(r):
        @pl.when(has_far)
        def _():
            arrived(r, far, 1)
            flow_copy(5, r).start()
            flow_copy(6, r).start()

        @pl.when(has_close)
        def _():
            arrived(r, close, 1)
            flow_copy(7, r).start()

    first_energy = a * energy_count
    top = energies * energy_count

    def stage(r):
        arrived(r, OWN, 1 - step)

        @pl.when(has_far)
        def _():
            arrived(r, far, 1 - step)

        @pl.when(has_close)
        def _():
            arrived(r, close, 0)
            arrived(r, close, 2)

        own_copies[r].wait()
        buf = bufs[r]
        span = modes * 2 * rows

        def k_step(k, _):
            place = jnp.clip(near_ref[0, k] - s + 1, 0, 2)
            for m in range(modes):
                shift = shift_ref[m]
                count = occ_ref[m]
                pieces = []
                for e in range(energy_count):
                    energy = first_energy + e
                    more = jnp.where(energy + shift < top, count + 1.0, 0.0)
                    less = jnp.where(energy - shift >= 0, count, 0.0)
                    above, below = energy_count + e + shift, energy_count + e - shift
                    pieces.append(
                        jnp.concatenate(
                            [
                                more * buf[place, above, part] + less * buf[place, below, part]
                                for part in range(2)
                            ],
                            axis=1,
                        )
                    )
                high, low = halves(jnp.concatenate(pieces, axis=0))
                count_rows = energy_count * rows
                first = jnp.dot(
                    jnp.concatenate([high, low], axis=0),
                    adjoint_high[m, k],
                    preferred_element_type=jnp.float32,
                )
                second = jnp.dot(high, adjoint_low[m, k], preferred_element_type=jnp.float32)
                result = first[:count_rows] + first[count_rows:] + second
                for e in range(energy_count):
                    part = result[e * rows : (e + 1) * rows]
                    turned = jnp.concatenate([-part[:, size:], part[:, :size]], axis=1)
                    base = m * 2 * rows
                    columns = slice(e * 2 * size, (e + 1) * 2 * size)
                    for offset, value in ((0, part), (rows, turned)):
                        high_value, low_value = halves(value)
                        middle_high[base + offset : base + offset + rows, columns] = high_value
                        middle_low[base + offset : base + offset + rows, columns] = low_value
            lhs = left[r, k]
            both = jnp.dot(lhs, middle_high[...], preferred_element_type=jnp.float32)
            rest = jnp.dot(lhs[:size], middle_low[...], preferred_element_type=jnp.float32)
            total[...] += both[:size] + both[size:] + rest
            return 0

        lax.fori_loop(0, ks, k_step, 0)

    total[...] = jnp.zeros_like(total)
    prepare()

    @pl.when((layer == 0) & has_far)
    def _():
        pl.semaphore_wait(ready_sem, 1)
        for r in range(AHEAD):
            flow_copy(2, r).start()

    for r in range(CHUNKS):
        relay_far(r)
        if r >= 1:
            relay_close(r - 1)
        if r >= 2:
            stage(r - 2)
    relay_close(CHUNKS - 1)
    stage(CHUNKS - 2)
    stage(CHUNKS - 1)
    for e in range(energy_count):
        for part in range(2):
            start = (2 * e + part) * size
            out_ref[e, 0, part] = total[:, start : start + size]
    for r in range(CHUNKS):
        for flow in (0, 1):
            flow_copy(flow, r).wait_send()

        @pl.when(has_far)
        def _():
            for flow in range(2, 7):
                flow_copy(flow, r).wait_send()

        @pl.when(has_close)
        def _():
            flow_copy(7, r).wait_send()


def solution(mesh):
    energies, slabs = mesh.shape["energy"], mesh.shape["slab"]

    def shards(green_lesser, coupling, occupation, shifts, neighbours):
        energy_count, _, _, size, _ = green_lesser.shape
        modes, _, ks = coupling.shape[:3]
        rows = size // CHUNKS
        bf16, f32 = jnp.bfloat16, jnp.float32
        smem = pl.BlockSpec(memory_space=pltpu.SMEM)
        hbm = pl.BlockSpec(memory_space=pl.ANY)
        return pl.pallas_call(
            functools.partial(kernel, energy_count, energies, slabs),
            out_shape=jax.ShapeDtypeStruct(green_lesser.shape, f32),
            in_specs=[smem, smem, smem, hbm, hbm],
            out_specs=pl.BlockSpec(memory_space=pltpu.VMEM),
            scratch_shapes=[pltpu.VMEM((3, 3 * energy_count, 2, rows, size), f32) for _ in range(CHUNKS)]
            + [
                pltpu.VMEM(coupling.shape, f32),
                pltpu.VMEM((modes, ks, 2 * size, 2 * size), bf16),
                pltpu.VMEM((modes, ks, 2 * size, 2 * size), bf16),
                pltpu.VMEM((CHUNKS, ks, 2 * size, modes * 2 * rows), bf16),
                pltpu.VMEM((modes * 2 * rows, energy_count * 2 * size), bf16),
                pltpu.VMEM((modes * 2 * rows, energy_count * 2 * size), bf16),
                pltpu.VMEM((size, energy_count * 2 * size), f32),
                pltpu.SemaphoreType.DMA((8, CHUNKS)),
                pltpu.SemaphoreType.DMA((CHUNKS, 3, 3)),
                pltpu.SemaphoreType.DMA((CHUNKS,)),
                pltpu.SemaphoreType.DMA,
                pltpu.SemaphoreType.REGULAR,
            ],
            compiler_params=pltpu.CompilerParams(collective_id=0, has_side_effects=True),
        )(occupation, shifts, neighbours, green_lesser, coupling)

    return jax.shard_map(
        shards,
        mesh=mesh,
        in_specs=(
            P("energy", "slab", None, None, None),
            P(None, "slab", None, None, None, None),
            P(),
            P(),
            P("slab", None),
        ),
        out_specs=P("energy", "slab", None, None, None),
        check_vma=False,
    )
```

time: 142 us -> 40 us (0.28)
  the two profiles are of different devices: /device:TPU:30 before, /device:TPU:2 now
where the time goes in v1:
time: 40 us; the launch traced here: 39.8 us
  Pallas kernels  38.2 us (96%)
  local copies, waits for them, and re-layouts  1.67 us (4%)
    pallas_call x1, Pallas kernels, shards(): pl.pallas_call(functools.partial(kernel, energy_count, energies, slabs),...  38.2 us
    unnamed x1, local copies, waits for them, and re-layouts  1.67 us

profile of v1, /device:TPU:2, one launch (start us, length us, event | category | flops | bytes accessed | tf_op | source)
XLA Modules:
  0.0 39.8 jit_solution(6594572615771398296)
XLA Ops:
  0.0 38.2 %shard_map.55 = f32[2,1,2,128,128]{4,3,2,1,0:T(8,128)} custom-call(f32[4]{0:T(128)} %occ_ref.1, s32[4]{0:T(128)} %shift_ref.1, s32[1,3]{1,0:T(1,128)} %near_ref.1, f32[2,1,2,128,128]{4,3,2,1,0:T(8,128)} %g_ref.1, f32[4,1,3,2,128,128]{5,4,3,2,1,0:T(8,128)} %c_ref.1), custom_call_target="tpu_custom_call" | custom-call | tf_op jit(solution)/shard_map/pallas_call | solution.py:278
  38.2 1.7 %copy.7 = f32[2,1,2,128,128]{4,3,2,1,0:T(8,128)} copy(f32[2,1,2,128,128]{4,3,2,1,0:T(8,128)} %shard_map.55) | data formatting | bytes 524288

commit v2 on v1

v2 whole, which is shorter than its diff:
```python
import functools

import jax
import jax.numpy as jnp
from jax import lax
from jax.experimental import pallas as pl
from jax.experimental.pallas import tpu as pltpu
from jax.sharding import PartitionSpec as P

MESH = pl.DeviceIdType.MESH
ROWS = (64, 64)
STARTS = tuple(sum(ROWS[:r]) for r in range(len(ROWS)))
CHUNKS = len(ROWS)
AHEAD = 2
LAG = 2
OWN = 1
SPARE = 3


def halves(value):
    high = value.astype(jnp.bfloat16)
    return high, (value - high.astype(jnp.float32)).astype(jnp.bfloat16)


def kernel(energy_count, energies, slabs, occ_ref, shift_ref, near_ref, g_ref, c_ref, out_ref, *scratch):
    bufs, scratch = scratch[:CHUNKS], scratch[CHUNKS:]
    lefts, scratch = scratch[:CHUNKS], scratch[CHUNKS:]
    couple, adjoint_high, adjoint_low, middle_high, middle_low, total = scratch[:6]
    send_sem, recv_sem, own_sem, couple_sem, ready_sem = scratch[6:]
    modes, ks, size = c_ref.shape[0], c_ref.shape[2], c_ref.shape[-1]

    a, s = lax.axis_index("energy"), lax.axis_index("slab")
    core, layer = lax.rem(a, 2), lax.rem(lax.div(a, 2), 2)
    step = 2 * core - 1
    partner = a - step
    mate = a + 3 - 2 * lax.rem(a, 4)
    edge = core == layer
    onto, behind = a - 4 * step, a + 4 * step
    has_onto = edge & (onto >= 0) & (onto < energies)
    has_behind = edge & (behind >= 0) & (behind < energies)
    beside = a + step
    has_beside = (beside >= 0) & (beside < energies)
    across = jnp.where(layer == 0, s - 1, s + 1)
    opposite = 2 * s - across
    close = 2 - 2 * layer
    far = 2 * layer
    has_far = (across >= 0) & (across < slabs)
    has_close = (opposite >= 0) & (opposite < slabs)
    inner, outer = 1 - step, 1 + step
    mine, theirs = jnp.where(edge, SPARE, outer), jnp.where(edge, SPARE, inner)

    def own_block(r):
        return g_ref.at[:, 0, :, pl.ds(STARTS[r], ROWS[r]), :]

    def slot(r, side, place):
        return bufs[r].at[side, pl.ds(energy_count * place, energy_count)]

    def remote(flow, r, source, side, place, target):
        return pltpu.make_async_remote_copy(
            src_ref=source,
            dst_ref=slot(r, side, place),
            send_sem=send_sem.at[flow, r],
            recv_sem=recv_sem.at[r, side, place],
            device_id={"energy": target[0], "slab": target[1]},
            device_id_type=MESH,
        )

    def flow_copy(flow, r):
        own = own_block(r)
        table = (
            (own, OWN, theirs, (mate, s)),
            (own, OWN, outer, (partner, s)),
            (own, close, theirs, (mate, across)),
            (slot(r, OWN, mine), close, 1, (mate, across)),
            (slot(r, far, mine), far, 1, (mate, s)),
            (slot(r, far, 1), far, inner, (beside, s)),
            (slot(r, far, 1), far, outer, (partner, s)),
            (slot(r, close, 1), close, outer, (partner, s)),
            (slot(r, OWN, SPARE), OWN, outer, (onto, s)),
            (slot(r, far, SPARE), far, outer, (onto, s)),
        )
        return remote(flow, r, *table[flow])

    def send(flow, r):
        flow_copy(flow, r).start()

    def arrived(r, side, place):
        remote(0, r, slot(r, side, place), side, place, (mate, s)).wait_recv()

    def signal(semaphore, target):
        pl.semaphore_signal(
            semaphore, inc=1, device_id={"energy": target[0], "slab": target[1]}, device_id_type=MESH
        )

    barrier = pltpu.get_barrier_semaphore()
    signal(barrier, (mate, s))
    signal(barrier, (partner, s))

    @pl.when((layer == 0) & has_far)
    def _():
        signal(barrier, (mate, across))

    @pl.when(has_onto)
    def _():
        signal(barrier, (onto, s))

    @pl.when(has_behind)
    def _():
        signal(barrier, (behind, s))
        signal(barrier, (beside, s))

    couple_copy = pltpu.make_async_copy(c_ref, couple, couple_sem)
    couple_copy.start()
    own_copies = [
        pltpu.make_async_copy(own_block(r), slot(r, OWN, 1), own_sem.at[r]) for r in range(CHUNKS)
    ]
    for copy in own_copies:
        copy.start()
    pl.semaphore_wait(
        barrier,
        2
        + ((layer == 1) & has_far).astype(jnp.int32)
        + has_onto.astype(jnp.int32)
        + 2 * has_behind.astype(jnp.int32),
    )

    @pl.when((layer == 1) & has_far)
    def _():
        signal(ready_sem, (mate, across))
        for r in range(AHEAD):
            send(2, r)

    for r in range(CHUNKS):
        send(0, r)
        send(1, r)

    def prepare():
        couple_copy.wait()

        def mode_step(m, _):
            for k in range(ks):
                real_t, imag_t = couple[m, 0, k, 0].T, couple[m, 0, k, 1].T
                adjoint = jnp.concatenate(
                    [
                        jnp.concatenate([real_t, -imag_t], axis=1),
                        jnp.concatenate([imag_t, real_t], axis=1),
                    ],
                    axis=0,
                )
                adjoint_high[m, k], adjoint_low[m, k] = halves(adjoint)
            return 0

        lax.fori_loop(0, modes, mode_step, 0)
        for r in range(CHUNKS):
            for k in range(ks):
                stacked = jnp.concatenate(
                    [
                        couple[m, 0, k, part][:, STARTS[r] : STARTS[r] + ROWS[r]]
                        for m in range(modes)
                        for part in range(2)
                    ],
                    axis=1,
                )
                high, low = halves(stacked)
                lefts[r][k, :size] = high
                lefts[r][k, size:] = low

    def pass_own(r):
        arrived(r, OWN, mine)

        @pl.when(has_far)
        def _():
            send(3, r)
            if r + AHEAD < CHUNKS:
                send(2, r + AHEAD)

        @pl.when(has_onto)
        def _():
            send(8, r)

    def pass_mates(r):
        @pl.when(has_far)
        def _():
            arrived(r, far, mine)
            send(4, r)

        @pl.when(has_far & has_onto)
        def _():
            send(9, r)

    def pass_far(r):
        @pl.when(has_far)
        def _():
            arrived(r, far, 1)
            send(6, r)

        @pl.when(has_far & has_beside)
        def _():
            send(5, r)

    def pass_close(r):
        @pl.when(has_close)
        def _():
            arrived(r, close, 1)
            send(7, r)

    def gather(r):
        own_copies[r].wait()
        arrived(r, OWN, inner)

        @pl.when(has_behind)
        def _():
            arrived(r, OWN, outer)

        @pl.when(has_far)
        def _():
            arrived(r, far, inner)

        @pl.when(has_far & has_behind)
        def _():
            arrived(r, far, outer)

        @pl.when(has_close)
        def _():
            arrived(r, close, inner)

        @pl.when(has_close & has_beside)
        def _():
            arrived(r, close, outer)

    first_energy = a * energy_count
    top = energies * energy_count

    def multiply(r, low_k, high_k):
        buf, rows = bufs[r], ROWS[r]
        span = modes * 2 * rows

        def k_step(k, _):
            place = jnp.clip(near_ref[0, k] - s + 1, 0, 2)
            for m in range(modes):
                shift = shift_ref[m]
                count = occ_ref[m]
                pieces = []
                for e in range(energy_count):
                    energy = first_energy + e
                    more = jnp.where(energy + shift < top, count + 1.0, 0.0)
                    less = jnp.where(energy - shift >= 0, count, 0.0)
                    above, below = energy_count + e + shift, energy_count + e - shift
                    pieces.append(
                        jnp.concatenate(
                            [
                                more * buf[place, above, part] + less * buf[place, below, part]
                                for part in range(2)
                            ],
                            axis=1,
                        )
                    )
                high, low = halves(jnp.concatenate(pieces, axis=0))
                count_rows = energy_count * rows
                first = jnp.dot(
                    jnp.concatenate([high, low], axis=0),
                    adjoint_high[m, k],
                    preferred_element_type=jnp.float32,
                )
                second = jnp.dot(high, adjoint_low[m, k], preferred_element_type=jnp.float32)
                result = first[:count_rows] + first[count_rows:] + second
                for e in range(energy_count):
                    part = result[e * rows : (e + 1) * rows]
                    turned = jnp.concatenate([-part[:, size:], part[:, :size]], axis=1)
                    base = m * 2 * rows
                    columns = slice(e * 2 * size, (e + 1) * 2 * size)
                    for offset, value in ((0, part), (rows, turned)):
                        high_value, low_value = halves(value)
                        middle_high[base + offset : base + offset + rows, columns] = high_value
                        middle_low[base + offset : base + offset + rows, columns] = low_value
            lhs = lefts[r][k]
            both = jnp.dot(lhs, middle_high[:span], preferred_element_type=jnp.float32)
            rest = jnp.dot(lhs[:size], middle_low[:span], preferred_element_type=jnp.float32)
            total[...] += both[:size] + both[size:] + rest
            return 0

        lax.fori_loop(low_k, high_k, k_step, 0)

    prepare()
    total[...] = jnp.zeros_like(total)

    @pl.when(edge & ~has_behind)
    def _():
        for r in range(CHUNKS):
            for side in range(3):
                for e in range(energy_count):
                    bufs[r][side, energy_count * outer + e] = jnp.zeros((2, ROWS[r], size), jnp.float32)

    @pl.when((layer == 0) & has_far)
    def _():
        pl.semaphore_wait(ready_sem, 1)
        for r in range(AHEAD):
            send(2, r)

    for r in range(CHUNKS):
        pass_own(r)
    for r in range(CHUNKS):
        pass_mates(r)
    for r in range(CHUNKS + LAG):
        if r < CHUNKS:
            pass_far(r)
            pass_close(r)
        if r >= LAG:
            gather(r - LAG)
            multiply(r - LAG, 0, ks)
    for e in range(energy_count):
        for part in range(2):
            start = (2 * e + part) * size
            out_ref[e, 0, part] = total[:, start : start + size]

    for r in range(CHUNKS):
        for flows, sent in (
            ((0, 1), None),
            ((2, 3, 4, 6), has_far),
            ((5,), has_far & has_beside),
            ((7,), has_close),
            ((8,), has_onto),
            ((9,), has_far & has_onto),
        ):

            def finish(flows=flows, r=r):
                for flow in flows:
                    flow_copy(flow, r).wait_send()

            if sent is None:
                finish()
            else:
                pl.when(sent)(finish)


def solution(mesh):
    energies, slabs = mesh.shape["energy"], mesh.shape["slab"]

    def shards(green_lesser, coupling, occupation, shifts, neighbours):
        energy_count, _, _, size, _ = green_lesser.shape
        modes, _, ks = coupling.shape[:3]
        bf16, f32 = jnp.bfloat16, jnp.float32
        smem = pl.BlockSpec(memory_space=pltpu.SMEM)
        hbm = pl.BlockSpec(memory_space=pl.ANY)
        depth = modes * 2 * max(ROWS)
        return pl.pallas_call(
            functools.partial(kernel, energy_count, energies, slabs),
            out_shape=jax.ShapeDtypeStruct(green_lesser.shape, f32),
            in_specs=[smem, smem, smem, hbm, hbm],
            out_specs=pl.BlockSpec(memory_space=pltpu.VMEM),
            scratch_shapes=[pltpu.VMEM((3, 4 * energy_count, 2, rows, size), f32) for rows in ROWS]
            + [pltpu.VMEM((ks, 2 * size, modes * 2 * rows), bf16) for rows in ROWS]
            + [
                pltpu.VMEM(coupling.shape, f32),
                pltpu.VMEM((modes, ks, 2 * size, 2 * size), bf16),
                pltpu.VMEM((modes, ks, 2 * size, 2 * size), bf16),
                pltpu.VMEM((depth, energy_count * 2 * size), bf16),
                pltpu.VMEM((depth, energy_count * 2 * size), bf16),
                pltpu.VMEM((size, energy_count * 2 * size), f32),
                pltpu.SemaphoreType.DMA((10, CHUNKS)),
                pltpu.SemaphoreType.DMA((CHUNKS, 3, 4)),
                pltpu.SemaphoreType.DMA((CHUNKS,)),
                pltpu.SemaphoreType.DMA,
                pltpu.SemaphoreType.REGULAR,
            ],
            compiler_params=pltpu.CompilerParams(collective_id=0, has_side_effects=True),
        )(occupation, shifts, neighbours, green_lesser, coupling)

    return jax.shard_map(
        shards,
        mesh=mesh,
        in_specs=(
            P("energy", "slab", None, None, None),
            P(None, "slab", None, None, None, None),
            P(),
            P(),
            P("slab", None),
        ),
        out_specs=P("energy", "slab", None, None, None),
        check_vma=False,
    )
```

time: 40 us -> 33.6 us (0.84)
  the two profiles are of different devices: /device:TPU:2 before, /device:TPU:95 now
where the time goes in v2:
time: 33.6 us; the launch traced here: 33.4 us
  Pallas kernels  31.8 us (95%)
  local copies, waits for them, and re-layouts  1.67 us (5%)
    pallas_call x1, Pallas kernels, shards(): pl.pallas_call(functools.partial(kernel, energy_count, energies, slabs),...  31.8 us
    unnamed x1, local copies, waits for them, and re-layouts  1.67 us

profile of v2, /device:TPU:95, one launch (start us, length us, event | category | flops | bytes accessed | tf_op | source)
XLA Modules:
  0.0 33.4 jit_solution(237696305988014034)
XLA Ops:
  0.0 31.8 %shard_map.55 = f32[2,1,2,128,128]{4,3,2,1,0:T(8,128)} custom-call(f32[4]{0:T(128)} %occ_ref.1, s32[4]{0:T(128)} %shift_ref.1, s32[1,3]{1,0:T(1,128)} %near_ref.1, f32[2,1,2,128,128]{4,3,2,1,0:T(8,128)} %g_ref.1, f32[4,1,3,2,128,128]{5,4,3,2,1,0:T(8,128)} %c_ref.1), custom_call_target="tpu_custom_call" | custom-call | tf_op jit(solution)/shard_map/pallas_call | solution.py:346
  31.8 1.7 %copy.7 = f32[2,1,2,128,128]{4,3,2,1,0:T(8,128)} copy(f32[2,1,2,128,128]{4,3,2,1,0:T(8,128)} %shard_map.55) | data formatting | bytes 524288

commit v3 on v2

--- a/solution.py
+++ b/solution.py
@@ -8,11 +8,11 @@
 from jax.sharding import PartitionSpec as P
 
 MESH = pl.DeviceIdType.MESH
-ROWS = (64, 64)
+ROWS = (32, 32, 32, 32)
 STARTS = tuple(sum(ROWS[:r]) for r in range(len(ROWS)))
 CHUNKS = len(ROWS)
-AHEAD = 2
-LAG = 2
+AHEAD = 4
+GROUPS = ((0, 1), (2, 3))
 OWN = 1
 SPARE = 3
 
@@ -22,11 +22,12 @@
     return high, (value - high.astype(jnp.float32)).astype(jnp.bfloat16)
 
 
-def kernel(energy_count, energies, slabs, occ_ref, shift_ref, near_ref, g_ref, c_ref, out_ref, *scratch):
+def kernel(energy_count, energies, slabs, occ_hbm, shift_hbm, near_hbm, g_ref, c_ref, out_ref, *scratch):
     bufs, scratch = scratch[:CHUNKS], scratch[CHUNKS:]
-    lefts, scratch = scratch[:CHUNKS], scratch[CHUNKS:]
+    lefts, scratch = scratch[: len(GROUPS)], scratch[len(GROUPS) :]
     couple, adjoint_high, adjoint_low, middle_high, middle_low, total = scratch[:6]
-    send_sem, recv_sem, own_sem, couple_sem, ready_sem = scratch[6:]
+    occ_ref, shift_ref, near_ref = scratch[6:9]
+    send_sem, recv_sem, own_sem, couple_sem, scalar_sem, ready_sem, go_sem = scratch[9:]
     modes, ks, size = c_ref.shape[0], c_ref.shape[2], c_ref.shape[-1]
 
     a, s = lax.axis_index("energy"), lax.axis_index("slab")
@@ -93,22 +94,47 @@
         )
 
     barrier = pltpu.get_barrier_semaphore()
-    signal(barrier, (mate, s))
-    signal(barrier, (partner, s))
-
-    @pl.when((layer == 0) & has_far)
-    def _():
-        signal(barrier, (mate, across))
-
-    @pl.when(has_onto)
-    def _():
-        signal(barrier, (onto, s))
-
-    @pl.when(has_behind)
-    def _():
-        signal(barrier, (behind, s))
-        signal(barrier, (beside, s))
-
+    upper, lower = layer == 1, layer == 0
+
+    @pl.when(lower)
+    def _():
+        signal(barrier, (partner, s))
+
+        @pl.when(has_far)
+        def _():
+            signal(barrier, (mate, across))
+
+        @pl.when(has_onto)
+        def _():
+            signal(barrier, (onto, s))
+
+        @pl.when(has_behind)
+        def _():
+            signal(barrier, (behind, s))
+            signal(barrier, (behind, s))
+
+    @pl.when(upper)
+    def _():
+        signal(barrier, (mate, s))
+        signal(barrier, (mate + step, s))
+
+        @pl.when(has_onto)
+        def _():
+            signal(barrier, (mate + onto - a, s))
+
+        @pl.when(has_behind)
+        def _():
+            signal(barrier, (mate + behind - a, s))
+            signal(barrier, (beside, s))
+
+    scalar_copies = [
+        pltpu.make_async_copy(source, target, scalar_sem.at[n])
+        for n, (source, target) in enumerate(
+            ((occ_hbm, occ_ref), (shift_hbm, shift_ref), (near_hbm, near_ref))
+        )
+    ]
+    for copy in scalar_copies:
+        copy.start()
     couple_copy = pltpu.make_async_copy(c_ref, couple, couple_sem)
     couple_copy.start()
     own_copies = [
@@ -116,19 +142,24 @@
     ]
     for copy in own_copies:
         copy.start()
-    pl.semaphore_wait(
-        barrier,
-        2
-        + ((layer == 1) & has_far).astype(jnp.int32)
-        + has_onto.astype(jnp.int32)
-        + 2 * has_behind.astype(jnp.int32),
-    )
-
-    @pl.when((layer == 1) & has_far)
+    @pl.when(lower | has_far)
+    def _():
+        told = 3 + 3 * (has_onto.astype(jnp.int32) + has_behind.astype(jnp.int32))
+        pl.semaphore_wait(barrier, jnp.where(upper, 1, told))
+
+    @pl.when(upper & has_far)
     def _():
         signal(ready_sem, (mate, across))
         for r in range(AHEAD):
             send(2, r)
+
+    @pl.when(lower)
+    def _():
+        signal(go_sem, (mate, s))
+
+    @pl.when(upper)
+    def _():
+        pl.semaphore_wait(go_sem, 1)
 
     for r in range(CHUNKS):
         send(0, r)
@@ -151,19 +182,20 @@
             return 0
 
         lax.fori_loop(0, modes, mode_step, 0)
-        for r in range(CHUNKS):
+        for n, group in enumerate(GROUPS):
+            first, last = STARTS[group[0]], STARTS[group[-1]] + ROWS[group[-1]]
             for k in range(ks):
                 stacked = jnp.concatenate(
                     [
-                        couple[m, 0, k, part][:, STARTS[r] : STARTS[r] + ROWS[r]]
+                        couple[m, 0, k, part][:, first:last]
                         for m in range(modes)
                         for part in range(2)
                     ],
                     axis=1,
                 )
                 high, low = halves(stacked)
-                lefts[r][k, :size] = high
-                lefts[r][k, size:] = low
+                lefts[n][k, :size] = high
+                lefts[n][k, size:] = low
 
     def pass_own(r):
         arrived(r, OWN, mine)
@@ -231,8 +263,9 @@
     first_energy = a * energy_count
     top = energies * energy_count
 
-    def multiply(r, low_k, high_k):
-        buf, rows = bufs[r], ROWS[r]
+    def multiply(n):
+        group = GROUPS[n]
+        rows = sum(ROWS[r] for r in group)
         span = modes * 2 * rows
 
         def k_step(k, _):
@@ -246,15 +279,17 @@
                     more = jnp.where(energy + shift < top, count + 1.0, 0.0)
                     less = jnp.where(energy - shift >= 0, count, 0.0)
                     above, below = energy_count + e + shift, energy_count + e - shift
-                    pieces.append(
-                        jnp.concatenate(
-                            [
-                                more * buf[place, above, part] + less * buf[place, below, part]
-                                for part in range(2)
-                            ],
-                            axis=1,
+                    for r in group:
+                        pieces.append(
+                            jnp.concatenate(
+                                [
+                                    more * bufs[r][place, above, part]
+                                    + less * bufs[r][place, below, part]
+                                    for part in range(2)
+                                ],
+                                axis=1,
+                            )
                         )
-                    )
                 high, low = halves(jnp.concatenate(pieces, axis=0))
                 count_rows = energy_count * rows
                 first = jnp.dot(
@@ -273,14 +308,22 @@
                         high_value, low_value = halves(value)
                         middle_high[base + offset : base + offset + rows, columns] = high_value
                         middle_low[base + offset : base + offset + rows, columns] = low_value
-            lhs = lefts[r][k]
+            lhs = lefts[n][k]
             both = jnp.dot(lhs, middle_high[:span], preferred_element_type=jnp.float32)
             rest = jnp.dot(lhs[:size], middle_low[:span], preferred_element_type=jnp.float32)
             total[...] += both[:size] + both[size:] + rest
             return 0
 
-        lax.fori_loop(low_k, high_k, k_step, 0)
-
+        lax.fori_loop(0, ks, k_step, 0)
+
+    @pl.when((layer == 0) & has_far)
+    def _():
+        pl.semaphore_wait(ready_sem, 1)
+        for r in range(AHEAD):
+            send(2, r)
+
+    for copy in scalar_copies:
+        copy.wait()
     prepare()
     total[...] = jnp.zeros_like(total)
 
@@ -291,23 +334,26 @@
                 for e in range(energy_count):
                     bufs[r][side, energy_count * outer + e] = jnp.zeros((2, ROWS[r], size), jnp.float32)
 
-    @pl.when((layer == 0) & has_far)
-    def _():
-        pl.semaphore_wait(ready_sem, 1)
-        for r in range(AHEAD):
-            send(2, r)
-
-    for r in range(CHUNKS):
-        pass_own(r)
-    for r in range(CHUNKS):
-        pass_mates(r)
-    for r in range(CHUNKS + LAG):
-        if r < CHUNKS:
-            pass_far(r)
-            pass_close(r)
-        if r >= LAG:
-            gather(r - LAG)
-            multiply(r - LAG, 0, ks)
+    pass_own(0)
+    pass_own(1)
+    pass_mates(0)
+    pass_own(2)
+    pass_mates(1)
+    pass_own(3)
+    pass_mates(2)
+    pass_mates(3)
+    pass_far(0)
+    pass_far(1)
+    pass_far(2)
+    pass_far(3)
+    pass_close(0)
+    pass_close(1)
+    pass_close(2)
+    pass_close(3)
+    for n, group in enumerate(GROUPS):
+        for r in group:
+            gather(r)
+        multiply(n)
     for e in range(energy_count):
         for part in range(2):
             start = (2 * e + part) * size
@@ -340,16 +386,16 @@
         energy_count, _, _, size, _ = green_lesser.shape
         modes, _, ks = coupling.shape[:3]
         bf16, f32 = jnp.bfloat16, jnp.float32
-        smem = pl.BlockSpec(memory_space=pltpu.SMEM)
         hbm = pl.BlockSpec(memory_space=pl.ANY)
-        depth = modes * 2 * max(ROWS)
-        return pl.pallas_call(
+        spans = [modes * 2 * sum(ROWS[r] for r in group) for group in GROUPS]
+        depth = max(spans)
+        total = pl.pallas_call(
             functools.partial(kernel, energy_count, energies, slabs),
-            out_shape=jax.ShapeDtypeStruct(green_lesser.shape, f32),
-            in_specs=[smem, smem, smem, hbm, hbm],
+            out_shape=pltpu.VMEM(green_lesser.shape, f32),
+            in_specs=[hbm] * 5,
             out_specs=pl.BlockSpec(memory_space=pltpu.VMEM),
             scratch_shapes=[pltpu.VMEM((3, 4 * energy_count, 2, rows, size), f32) for rows in ROWS]
-            + [pltpu.VMEM((ks, 2 * size, modes * 2 * rows), bf16) for rows in ROWS]
+            + [pltpu.VMEM((ks, 2 * size, span), bf16) for span in spans]
             + [
                 pltpu.VMEM(coupling.shape, f32),
                 pltpu.VMEM((modes, ks, 2 * size, 2 * size), bf16),
@@ -357,14 +403,20 @@
                 pltpu.VMEM((depth, energy_count * 2 * size), bf16),
                 pltpu.VMEM((depth, energy_count * 2 * size), bf16),
                 pltpu.VMEM((size, energy_count * 2 * size), f32),
+                pltpu.SMEM(occupation.shape, f32),
+                pltpu.SMEM(shifts.shape, jnp.int32),
+                pltpu.SMEM(neighbours.shape, jnp.int32),
                 pltpu.SemaphoreType.DMA((10, CHUNKS)),
                 pltpu.SemaphoreType.DMA((CHUNKS, 3, 4)),
                 pltpu.SemaphoreType.DMA((CHUNKS,)),
                 pltpu.SemaphoreType.DMA,
+                pltpu.SemaphoreType.DMA((3,)),
+                pltpu.SemaphoreType.REGULAR,
                 pltpu.SemaphoreType.REGULAR,
             ],
             compiler_params=pltpu.CompilerParams(collective_id=0, has_side_effects=True),
         )(occupation, shifts, neighbours, green_lesser, coupling)
+        return total
 
     return jax.shard_map(
         shards,

time: 33.6 us -> 29.8 us (0.89)
  the two profiles are of different devices: /device:TPU:95 before, /device:TPU:31 now
where the time goes in v3:
time: 29.8 us; the launch traced here: 29.7 us
  Pallas kernels  29 us (97%)
  local copies, waits for them, and re-layouts  0.71 us (2%)
    pallas_call x1, Pallas kernels, shards(): pl.pallas_call(functools.partial(kernel, energy_count, energies, slabs),...  29 us
    unnamed x1, local copies, waits for them, and re-layouts  0.71 us

profile of v3, /device:TPU:31, one launch (start us, length us, event | category | flops | bytes accessed | tf_op | source)
XLA Modules:
  0.0 29.7 jit_solution(6090041719764119955)
XLA Ops:
  0.0 29.0 %shard_map.55 = f32[2,1,2,128,128]{4,3,2,1,0:T(8,128)S(1)} custom-call(f32[4]{0:T(128)} %occ_hbm.1, s32[4]{0:T(128)} %shift_hbm.1, s32[1,3]{1,0:T(1,128)} %near_hbm.1, f32[2,1,2,128,128]{4,3,2,1,0:T(8,128)} %g_ref.1, f32[4,1,3,2,128,128]{5,4,3,2,1,0:T(8,128)} %c_ref.1), custom_call_target="tpu_custom_call" | custom-call | tf_op jit(solution)/shard_map/pallas_call | solution.py:392
  29.0 0.7 %copy.7 = f32[2,1,2,128,128]{4,3,2,1,0:T(8,128)} copy(f32[2,1,2,128,128]{4,3,2,1,0:T(8,128)S(1)} %shard_map.55) | data formatting | bytes 524288

commit v4 on v3

--- a/solution.py
+++ b/solution.py
@@ -11,9 +11,10 @@
 ROWS = (32, 32, 32, 32)
 STARTS = tuple(sum(ROWS[:r]) for r in range(len(ROWS)))
 CHUNKS = len(ROWS)
+LAG = 1
 AHEAD = 4
 GROUPS = ((0, 1), (2, 3))
-OWN = 1
+OWN, FAR, CLOSE = range(3)
 SPARE = 3
 
 
@@ -23,7 +24,8 @@
 
 
 def kernel(energy_count, energies, slabs, occ_hbm, shift_hbm, near_hbm, g_ref, c_ref, out_ref, *scratch):
-    bufs, scratch = scratch[:CHUNKS], scratch[CHUNKS:]
+    bufs, scratch = scratch[: 3 * CHUNKS], scratch[3 * CHUNKS :]
+    picked, scratch = scratch[:CHUNKS], scratch[CHUNKS:]
     lefts, scratch = scratch[: len(GROUPS)], scratch[len(GROUPS) :]
     couple, adjoint_high, adjoint_low, middle_high, middle_low, total = scratch[:6]
     occ_ref, shift_ref, near_ref = scratch[6:9]
@@ -43,8 +45,8 @@
     has_beside = (beside >= 0) & (beside < energies)
     across = jnp.where(layer == 0, s - 1, s + 1)
     opposite = 2 * s - across
-    close = 2 - 2 * layer
-    far = 2 * layer
+    far_k = 2 * layer
+    close_k = 2 - far_k
     has_far = (across >= 0) & (across < slabs)
     has_close = (opposite >= 0) & (opposite < slabs)
     inner, outer = 1 - step, 1 + step
@@ -54,7 +56,7 @@
         return g_ref.at[:, 0, :, pl.ds(STARTS[r], ROWS[r]), :]
 
     def slot(r, side, place):
-        return bufs[r].at[side, pl.ds(energy_count * place, energy_count)]
+        return bufs[3 * r + side].at[pl.ds(energy_count * place, energy_count)]
 
     def remote(flow, r, source, side, place, target):
         return pltpu.make_async_remote_copy(
@@ -71,14 +73,14 @@
         table = (
             (own, OWN, theirs, (mate, s)),
             (own, OWN, outer, (partner, s)),
-            (own, close, theirs, (mate, across)),
-            (slot(r, OWN, mine), close, 1, (mate, across)),
-            (slot(r, far, mine), far, 1, (mate, s)),
-            (slot(r, far, 1), far, inner, (beside, s)),
-            (slot(r, far, 1), far, outer, (partner, s)),
-            (slot(r, close, 1), close, outer, (partner, s)),
+            (own, FAR, theirs, (mate, across)),
+            (slot(r, OWN, mine), FAR, 1, (mate, across)),
+            (slot(r, FAR, mine), CLOSE, 1, (mate, s)),
+            (slot(r, FAR, 1), CLOSE, inner, (beside, s)),
+            (slot(r, FAR, 1), FAR, outer, (partner, s)),
+            (slot(r, CLOSE, 1), CLOSE, outer, (partner, s)),
             (slot(r, OWN, SPARE), OWN, outer, (onto, s)),
-            (slot(r, far, SPARE), far, outer, (onto, s)),
+            (slot(r, FAR, SPARE), FAR, outer, (onto, s)),
         )
         return remote(flow, r, *table[flow])
 
@@ -213,7 +215,7 @@
     def pass_mates(r):
         @pl.when(has_far)
         def _():
-            arrived(r, far, mine)
+            arrived(r, FAR, mine)
             send(4, r)
 
         @pl.when(has_far & has_onto)
@@ -223,7 +225,7 @@
     def pass_far(r):
         @pl.when(has_far)
         def _():
-            arrived(r, far, 1)
+            arrived(r, FAR, 1)
             send(6, r)
 
         @pl.when(has_far & has_beside)
@@ -233,10 +235,10 @@
     def pass_close(r):
         @pl.when(has_close)
         def _():
-            arrived(r, close, 1)
+            arrived(r, CLOSE, 1)
             send(7, r)
 
-    def gather(r):
+    def gather_own(r):
         own_copies[r].wait()
         arrived(r, OWN, inner)
 
@@ -244,77 +246,69 @@
         def _():
             arrived(r, OWN, outer)
 
-        @pl.when(has_far)
-        def _():
-            arrived(r, far, inner)
-
-        @pl.when(has_far & has_behind)
-        def _():
-            arrived(r, far, outer)
-
-        @pl.when(has_close)
-        def _():
-            arrived(r, close, inner)
-
-        @pl.when(has_close & has_beside)
-        def _():
-            arrived(r, close, outer)
+    def gather_far(r):
+        arrived(r, FAR, inner)
+
+        @pl.when(has_behind)
+        def _():
+            arrived(r, FAR, outer)
+
+    def gather_close(r):
+        arrived(r, CLOSE, inner)
+
+        @pl.when(has_beside)
+        def _():
+            arrived(r, CLOSE, outer)
 
     first_energy = a * energy_count
     top = energies * energy_count
 
-    def multiply(n):
+    def multiply(n, sources, k):
         group = GROUPS[n]
         rows = sum(ROWS[r] for r in group)
         span = modes * 2 * rows
-
-        def k_step(k, _):
-            place = jnp.clip(near_ref[0, k] - s + 1, 0, 2)
-            for m in range(modes):
-                shift = shift_ref[m]
-                count = occ_ref[m]
-                pieces = []
-                for e in range(energy_count):
-                    energy = first_energy + e
-                    more = jnp.where(energy + shift < top, count + 1.0, 0.0)
-                    less = jnp.where(energy - shift >= 0, count, 0.0)
-                    above, below = energy_count + e + shift, energy_count + e - shift
-                    for r in group:
-                        pieces.append(
-                            jnp.concatenate(
-                                [
-                                    more * bufs[r][place, above, part]
-                                    + less * bufs[r][place, below, part]
-                                    for part in range(2)
-                                ],
-                                axis=1,
-                            )
+        for m in range(modes):
+            shift = shift_ref[m]
+            count = occ_ref[m]
+            pieces = []
+            for e in range(energy_count):
+                energy = first_energy + e
+                more = jnp.where(energy + shift < top, count + 1.0, 0.0)
+                less = jnp.where(energy - shift >= 0, count, 0.0)
+                above, below = energy_count + e + shift, energy_count + e - shift
+                for r in group:
+                    pieces.append(
+                        jnp.concatenate(
+                            [
+                                more * sources[r][above, part]
+                                + less * sources[r][below, part]
+                                for part in range(2)
+                            ],
+                            axis=1,
                         )
-                high, low = halves(jnp.concatenate(pieces, axis=0))
-                count_rows = energy_count * rows
-                first = jnp.dot(
-                    jnp.concatenate([high, low], axis=0),
-                    adjoint_high[m, k],
-                    preferred_element_type=jnp.float32,
-                )
-                second = jnp.dot(high, adjoint_low[m, k], preferred_element_type=jnp.float32)
-                result = first[:count_rows] + first[count_rows:] + second
-                for e in range(energy_count):
-                    part = result[e * rows : (e + 1) * rows]
-                    turned = jnp.concatenate([-part[:, size:], part[:, :size]], axis=1)
-                    base = m * 2 * rows
-                    columns = slice(e * 2 * size, (e + 1) * 2 * size)
-                    for offset, value in ((0, part), (rows, turned)):
-                        high_value, low_value = halves(value)
-                        middle_high[base + offset : base + offset + rows, columns] = high_value
-                        middle_low[base + offset : base + offset + rows, columns] = low_value
-            lhs = lefts[n][k]
-            both = jnp.dot(lhs, middle_high[:span], preferred_element_type=jnp.float32)
-            rest = jnp.dot(lhs[:size], middle_low[:span], preferred_element_type=jnp.float32)
-            total[...] += both[:size] + both[size:] + rest
-            return 0
-
-        lax.fori_loop(0, ks, k_step, 0)
+                    )
+            high, low = halves(jnp.concatenate(pieces, axis=0))
+            count_rows = energy_count * rows
+            first = jnp.dot(
+                jnp.concatenate([high, low], axis=0),
+                adjoint_high[m, k],
+                preferred_element_type=jnp.float32,
+            )
+            second = jnp.dot(high, adjoint_low[m, k], preferred_element_type=jnp.float32)
+            result = first[:count_rows] + first[count_rows:] + second
+            for e in range(energy_count):
+                part = result[e * rows : (e + 1) * rows]
+                turned = jnp.concatenate([-part[:, size:], part[:, :size]], axis=1)
+                base = m * 2 * rows
+                columns = slice(e * 2 * size, (e + 1) * 2 * size)
+                for offset, value in ((0, part), (rows, turned)):
+                    high_value, low_value = halves(value)
+                    middle_high[base + offset : base + offset + rows, columns] = high_value
+                    middle_low[base + offset : base + offset + rows, columns] = low_value
+        lhs = lefts[n][k]
+        both = jnp.dot(lhs, middle_high[:span], preferred_element_type=jnp.float32)
+        rest = jnp.dot(lhs[:size], middle_low[:span], preferred_element_type=jnp.float32)
+        total[...] += both[:size] + both[size:] + rest
 
     @pl.when((layer == 0) & has_far)
     def _():
@@ -330,30 +324,95 @@
     @pl.when(edge & ~has_behind)
     def _():
         for r in range(CHUNKS):
-            for side in range(3):
+            for side in (OWN, FAR, CLOSE):
                 for e in range(energy_count):
-                    bufs[r][side, energy_count * outer + e] = jnp.zeros((2, ROWS[r], size), jnp.float32)
-
-    pass_own(0)
-    pass_own(1)
-    pass_mates(0)
-    pass_own(2)
-    pass_mates(1)
-    pass_own(3)
-    pass_mates(2)
-    pass_mates(3)
-    pass_far(0)
-    pass_far(1)
-    pass_far(2)
-    pass_far(3)
-    pass_close(0)
-    pass_close(1)
-    pass_close(2)
-    pass_close(3)
-    for n, group in enumerate(GROUPS):
-        for r in group:
-            gather(r)
-        multiply(n)
+                    bufs[3 * r + side][energy_count * outer + e] = jnp.zeros((2, ROWS[r], size), jnp.float32)
+
+    for r in range(CHUNKS + LAG):
+        if r < CHUNKS:
+            pass_own(r)
+        if r >= LAG:
+            pass_mates(r - LAG)
+    def side_of(side):
+        return [bufs[3 * r + side] for r in range(CHUNKS)]
+
+    def multiply_far(n):
+        @pl.when(has_far)
+        def _():
+            for r in GROUPS[n]:
+                gather_far(r)
+            multiply(n, side_of(FAR), far_k)
+
+    def multiply_close(n):
+        @pl.when(has_close)
+        def _():
+            for r in GROUPS[n]:
+                gather_close(r)
+            multiply(n, side_of(CLOSE), close_k)
+
+    def multiply_own(n):
+        for r in GROUPS[n]:
+            gather_own(r)
+
+        @pl.when(~(has_far & has_close))
+        def _():
+            multiply(n, side_of(OWN), jnp.where(has_far, close_k, far_k))
+
+    def multiply_middle(n):
+        place = near_ref[0, 1] - s + 1
+        for r in GROUPS[n]:
+            for energy in range(3 * energy_count):
+                own, far, close = (bufs[3 * r + side][energy] for side in (OWN, FAR, CLOSE))
+                picked[r][energy] = jnp.where(place == 1, own, jnp.where(place == far_k, far, close))
+        multiply(n, picked, 1)
+
+    groups = range(len(GROUPS))
+    first = lax.rem(s, 4) == 0
+    waiting = first & (layer == 0)
+
+    @pl.when(waiting)
+    def _():
+        pass_far(0)
+        pass_far(1)
+        for r in (0, 1):
+            pass_close(r)
+        multiply_close(0)
+        pass_far(2)
+        multiply_own(0)
+        multiply_far(0)
+        pass_far(3)
+        for r in (2, 3):
+            pass_close(r)
+        multiply_middle(0)
+        multiply_close(1)
+        multiply_own(1)
+        multiply_far(1)
+        multiply_middle(1)
+
+    @pl.when(~waiting)
+    def _():
+        for r in range(CHUNKS):
+            pass_far(r)
+        for r in range(CHUNKS):
+            pass_close(r)
+        far_last = ~first & (layer == 1)
+
+        @pl.when(far_last)
+        def _():
+            for n in groups:
+                multiply_close(n)
+
+        @pl.when(~far_last)
+        def _():
+            for n in groups:
+                multiply_far(n)
+
+        for n in groups:
+            multiply_own(n)
+            pl.when(far_last)(functools.partial(multiply_far, n))
+            pl.when(~far_last)(functools.partial(multiply_close, n))
+            multiply_middle(n)
+
     for e in range(energy_count):
         for part in range(2):
             start = (2 * e + part) * size
@@ -394,7 +453,10 @@
             out_shape=pltpu.VMEM(green_lesser.shape, f32),
             in_specs=[hbm] * 5,
             out_specs=pl.BlockSpec(memory_space=pltpu.VMEM),
-            scratch_shapes=[pltpu.VMEM((3, 4 * energy_count, 2, rows, size), f32) for rows in ROWS]
+            scratch_shapes=[
+                pltpu.VMEM((4 * energy_count, 2, rows, size), f32) for rows in ROWS for _ in range(3)
+            ]
+            + [pltpu.VMEM((3 * energy_count, 2, rows, size), f32) for rows in ROWS]
             + [pltpu.VMEM((ks, 2 * size, span), bf16) for span in spans]
             + [
                 pltpu.VMEM(coupling.shape, f32),

time: 29.8 us -> 29.8 us (level)
  the two profiles are of different devices: /device:TPU:31 before, /device:TPU:95 now
where the time goes in v4:
time: 29.8 us; the launch traced here: 29.6 us
  Pallas kernels  28.9 us (97%)
  local copies, waits for them, and re-layouts  0.71 us (2%)
    pallas_call x1, Pallas kernels, shards(): pl.pallas_call(functools.partial(kernel, energy_count, energies, slabs),...  28.9 us
    unnamed x1, local copies, waits for them, and re-layouts  0.71 us

profile of v4, /device:TPU:95, one launch (start us, length us, event | category | flops | bytes accessed | tf_op | source)
XLA Modules:
  0.0 29.6 jit_solution(3464151736124745735)
XLA Ops:
  0.0 28.9 %shard_map.55 = f32[2,1,2,128,128]{4,3,2,1,0:T(8,128)S(1)} custom-call(f32[4]{0:T(128)} %occ_hbm.1, s32[4]{0:T(128)} %shift_hbm.1, s32[1,3]{1,0:T(1,128)} %near_hbm.1, f32[2,1,2,128,128]{4,3,2,1,0:T(8,128)} %g_ref.1, f32[4,1,3,2,128,128]{5,4,3,2,1,0:T(8,128)} %c_ref.1), custom_call_target="tpu_custom_call" | custom-call | tf_op jit(solution)/shard_map/pallas_call | solution.py:451
  28.9 0.7 %copy.7 = f32[2,1,2,128,128]{4,3,2,1,0:T(8,128)} copy(f32[2,1,2,128,128]{4,3,2,1,0:T(8,128)S(1)} %shard_map.55) | data formatting | bytes 524288

commit v5 on v4

--- a/solution.py
+++ b/solution.py
@@ -129,6 +129,17 @@
             signal(barrier, (mate + behind - a, s))
             signal(barrier, (beside, s))
 
+    @pl.when(lower | has_far)
+    def _():
+        told = 3 + 3 * (has_onto.astype(jnp.int32) + has_behind.astype(jnp.int32))
+        pl.semaphore_wait(barrier, jnp.where(upper, 1, told))
+
+    @pl.when(upper & has_far)
+    def _():
+        signal(ready_sem, (mate, across))
+        for r in range(AHEAD):
+            send(2, r)
+
     scalar_copies = [
         pltpu.make_async_copy(source, target, scalar_sem.at[n])
         for n, (source, target) in enumerate(
@@ -144,17 +155,6 @@
     ]
     for copy in own_copies:
         copy.start()
-    @pl.when(lower | has_far)
-    def _():
-        told = 3 + 3 * (has_onto.astype(jnp.int32) + has_behind.astype(jnp.int32))
-        pl.semaphore_wait(barrier, jnp.where(upper, 1, told))
-
-    @pl.when(upper & has_far)
-    def _():
-        signal(ready_sem, (mate, across))
-        for r in range(AHEAD):
-            send(2, r)
-
     @pl.when(lower)
     def _():
         signal(go_sem, (mate, s))

time: 29.8 us -> 29.6 us (level)
  no operation moved by 1% of the time
where the time goes in v5:
time: 29.6 us; the launch traced here: 29.4 us
  Pallas kernels  28.7 us (97%)
  local copies, waits for them, and re-layouts  0.71 us (2%)
    pallas_call x1, Pallas kernels, shards(): pl.pallas_call(functools.partial(kernel, energy_count, energies, slabs),...  28.7 us
    unnamed x1, local copies, waits for them, and re-layouts  0.71 us

profile of v5, /device:TPU:95, one launch (start us, length us, event | category | flops | bytes accessed | tf_op | source)
XLA Modules:
  0.0 29.4 jit_solution(9287920326154889993)
XLA Ops:
  0.0 28.7 %shard_map.55 = f32[2,1,2,128,128]{4,3,2,1,0:T(8,128)S(1)} custom-call(f32[4]{0:T(128)} %occ_hbm.1, s32[4]{0:T(128)} %shift_hbm.1, s32[1,3]{1,0:T(1,128)} %near_hbm.1, f32[2,1,2,128,128]{4,3,2,1,0:T(8,128)} %g_ref.1, f32[4,1,3,2,128,128]{5,4,3,2,1,0:T(8,128)} %c_ref.1), custom_call_target="tpu_custom_call" | custom-call | tf_op jit(solution)/shard_map/pallas_call | solution.py:451
  28.7 0.7 %copy.7 = f32[2,1,2,128,128]{4,3,2,1,0:T(8,128)} copy(f32[2,1,2,128,128]{4,3,2,1,0:T(8,128)S(1)} %shard_map.55) | data formatting | bytes 524288
